TPU v7x, 256 devices: a whole 4x4x8 slice. The times are simulated.
256 devices in a mesh: grp: 8 (over y, core), sub: 32 (over x, z).
Axes of the slice: x: 4, y: 4, z: 8, core: 2. Of those that a mesh axis runs over, the one named last changes fastest.
Arguments:
- cluster_pos: float32 [3, 4096], P(None, 'sub'), may hold values from -3 to 3
- cluster_vel: float32 [3, 4096], P(None, 'sub'), may hold values from -15 to 15
- cluster_mass: float32 [4096], P('sub'), may hold values from 3 to 60
- galaxy_pos: float32 [3, 131072], P(None, ('grp', 'sub')), may hold values from -1 to 7
- galaxy_vel: float32 [3, 131072], P(None, ('grp', 'sub')), may hold values from -3 to 3
- galaxy_kind: int32 [131072], P(('grp', 'sub')), may hold values from 0 to 3
- species_mass: float32 [4], replicated, may hold values from 10 to 80
Outputs:
- cluster_pos_out: float32 [3, 4096], P(None, 'sub')
- cluster_vel_out: float32 [3, 4096], P(None, 'sub')
- galaxy_pos_out: float32 [3, 131072], P(None, ('grp', 'sub'))
- galaxy_vel_out: float32 [3, 131072], P(None, ('grp', 'sub'))
All inputs are finite; a program needn't handle non-finite values.
Results may differ from a plain program's by a relative error of at most 0.0003.
Values sent between devices are 32-bit elements; how exact they have to be, the bound alone decides.
A program may use at most 64 MiB of HBM per device.

v0:
```python
import jax
import jax.numpy as jnp
from jax import lax
from jax.sharding import PartitionSpec as P

SUBSTEPS = 8
step_time = 0.5
bridge_soft = 0.01
cluster_soft = 0.0025
tile_limit = 524288


def pick_block(target_count, source_count):
    tile_size = target_count
    while tile_size > 1 and (
        tile_size * source_count > tile_limit or target_count % tile_size != 0
    ):
        tile_size = tile_size // 2
    return tile_size


def field(targets, sources, masses, soften):
    target_count = targets.shape[1]
    tile_size = pick_block(target_count, sources.shape[1])

    def field_one_tile(target_tile):
        separation = sources[:, None, :] - target_tile[:, :, None]
        distance = jnp.sum(separation * separation, axis=0) + soften
        inverse = lax.rsqrt(distance)
        weight = masses[None, :] * inverse * inverse * inverse
        return jnp.sum(separation * weight[None], axis=2)

    stacked = targets.reshape(3, target_count // tile_size, tile_size).transpose(1, 0, 2)
    result = lax.map(field_one_tile, stacked)
    return result.transpose(1, 0, 2).reshape(3, target_count)


def rates(target_pos, target_vel, source_pos, source_vel, masses, soften):
    target_count = target_pos.shape[1]
    tile_size = pick_block(target_count, source_pos.shape[1])

    def rates_one_tile(target_tile):
        separation = source_pos[:, None, :] - target_tile[:3, :, None]
        closing = source_vel[:, None, :] - target_tile[3:, :, None]
        distance = jnp.sum(separation * separation, axis=0) + soften
        inverse = lax.rsqrt(distance)
        weight = masses[None, :] * inverse * inverse * inverse
        radial = 3.0 * jnp.sum(separation * closing, axis=0) / distance
        acceleration = jnp.sum(separation * weight[None], axis=2)
        jerk_rate = jnp.sum((closing - radial[None] * separation) * weight[None], axis=2)
        return jnp.concatenate([acceleration, jerk_rate], axis=0)

    stacked = jnp.concatenate([target_pos, target_vel], axis=0)
    stacked = stacked.reshape(6, target_count // tile_size, tile_size).transpose(1, 0, 2)
    result = lax.map(rates_one_tile, stacked)
    return result.transpose(1, 0, 2).reshape(6, target_count)


def local(
    cluster_pos, cluster_vel, cluster_mass, galaxy_pos, galaxy_vel, galaxy_kind, species_mass
):
    star_count = cluster_pos.shape[1]
    member_count = lax.axis_size("sub")
    group_count = lax.axis_size("grp")
    total_stars = star_count * member_count
    total_bodies = galaxy_pos.shape[1] * member_count * group_count
    star_mass = cluster_mass / total_stars
    species = jnp.arange(species_mass.shape[0], dtype=jnp.int32)
    body_mass = (
        jnp.sum(
            jnp.where(galaxy_kind[None, :] == species[:, None], species_mass[:, None], 0.0), axis=0
        )
        / total_bodies
    )
    half_step = step_time / 2.0

    def kick(star_positions, body_positions):
        stacked = jnp.concatenate([star_positions, star_mass[None, :]], axis=0)
        gathered = lax.all_gather(stacked, "sub", axis=1, tiled=True)
        galaxy_push = field(body_positions, gathered[:3], gathered[3], bridge_soft)
        partial_value = field(gathered[:3], body_positions, body_mass, bridge_soft)
        summed = lax.psum(partial_value, ("grp", "sub"))
        cluster_pull = lax.dynamic_slice_in_dim(
            summed, lax.axis_index("sub") * star_count, star_count, 1
        )
        return (cluster_pull, galaxy_push)

    def evaluate(guess_pos, guess_vel):
        sources = jnp.concatenate([guess_pos, guess_vel, star_mass[None, :]], axis=0)
        target_pos, target_vel = (guess_pos, guess_vel)
        source_piece = lax.all_gather(sources, "sub", axis=1, tiled=True)
        result = rates(
            target_pos,
            target_vel,
            source_piece[:3],
            source_piece[3:6],
            source_piece[6],
            cluster_soft,
        )
        return (result[:3], result[3:])

    first_pull, first_push = kick(cluster_pos, galaxy_pos)
    star_vel = cluster_vel + half_step * first_pull
    body_vel = galaxy_vel + half_step * first_push
    body_pos = galaxy_pos + step_time * body_vel
    substep_time = step_time / SUBSTEPS
    positions, velocity = (cluster_pos, star_vel)
    acceleration, jerk_rate = evaluate(positions, velocity)
    for substep in range(SUBSTEPS):
        guess_pos = positions + substep_time * (
            velocity + substep_time * (acceleration / 2.0 + substep_time * jerk_rate / 6.0)
        )
        guess_vel = velocity + substep_time * (acceleration + substep_time * jerk_rate / 2.0)
        new_acc, new_jerk = evaluate(guess_pos, guess_vel)
        new_vel = (
            velocity
            + substep_time / 2.0 * (acceleration + new_acc)
            + substep_time * substep_time / 12.0 * (jerk_rate - new_jerk)
        )
        new_pos = (
            positions
            + substep_time / 2.0 * (velocity + new_vel)
            + substep_time * substep_time / 12.0 * (acceleration - new_acc)
        )
        positions, velocity, acceleration, jerk_rate = (new_pos, new_vel, new_acc, new_jerk)
    second_pull, second_push = kick(positions, body_pos)
    return (
        positions,
        velocity + half_step * second_pull,
        body_pos,
        body_vel + half_step * second_push,
    )


def solution(mesh):
    return jax.shard_map(
        local,
        mesh=mesh,
        in_specs=(
            P(None, "sub"),
            P(None, "sub"),
            P("sub"),
            P(None, ("grp", "sub")),
            P(None, ("grp", "sub")),
            P(("grp", "sub")),
            P(),
        ),
        out_specs=(
            P(None, "sub"),
            P(None, "sub"),
            P(None, ("grp", "sub")),
            P(None, ("grp", "sub")),
        ),
        check_vma=False,
    )
```

profile of v0, /device:TPU:1, one launch (start us, length us, event | category | flops | bytes accessed | tf_op | source)
XLA Modules:
  0.0 715.4 jit_solution(4176489332510097580)
XLA Ops:
  2.0 40.5 %all_gather.33 = f32[4,4096]{1,0:T(4,128)S(1)} all-gather(f32[4,128]{1,0:T(4,128)S(1)} %pad_maximum_fusion.10), channel_id=1, replica_groups=mesh['grp'=8,'sub'=32] {'sub'}, dimensions={1}, use_global_device_ids=true | all-gather | bytes 67584 | tf_op jit(solution)/shard_map/all_gather | solution.py:79
  43.3 14.5 %while.8 = (s32[]{:T(128)}, f32[4,3,1024]{2,1,0:T(4,128)S(1)}, f32[3,512]{1,0:T(4,128)}, f32[4,3,1024]{2,1,0:T(4,128)S(1)}, f32[512]{0:T(512)S(1)}, /*index=5*/s32[]{:T(128)}) while((s32[]{:T(128)}, f32[4,3,1024]{2,1,0:T(4,128)S(1)}, f32[3,512]{1,0:T(4,128)}, f32[4,3,1024]{2,1,0:T(4,128)S(1)}, f32[512]{0:T(512)S(1)}, ...), condition=%wide.region_4.5_spmd, body=%wide.region_1.4_spmd.sunk | while | flops 11006978 | bytes 8521833 | solution.py:34
  57.8 87.6 %psum.14 = f32[3,4096]{1,0:T(4,128)S(1)} all-reduce(f32[3,4096]{1,0:T(4,128)S(1)} %bitcast.93), channel_id=1, replica_groups=mesh['grp'=8,'sub'=32] {'grp','sub'}, use_global_device_ids=true, to_apply=%region_5.6 | all-reduce | flops 12288 | bytes 98304 | tf_op jit(solution)/shard_map/psum | solution.py:82
  145.4 31.0 %all_gather.34 = f32[7,4096]{1,0:T(8,128)S(1)} all-gather(f32[7,128]{1,0:T(8,128)S(1)} %pad_maximum_fusion.8), channel_id=1, replica_groups=mesh['grp'=8,'sub'=32] {'sub'}, dimensions={1}, use_global_device_ids=true | all-gather | bytes 118272 | tf_op jit(solution)/shard_map/all_gather | solution.py:91
  181.2 32.3 %all_gather.35 = f32[7,4096]{1,0:T(8,128)S(1)} all-gather(f32[7,128]{1,0:T(8,128)S(1)} %pad_maximum_fusion.7), channel_id=1, replica_groups=mesh['grp'=8,'sub'=32] {'sub'}, dimensions={1}, use_global_device_ids=true | all-gather | bytes 118272 | tf_op jit(solution)/shard_map/all_gather | solution.py:91
  216.2 2.2 fusion.11
  218.4 31.8 %all_gather.36 = f32[7,4096]{1,0:T(8,128)S(1)} all-gather(f32[7,128]{1,0:T(8,128)S(1)} %pad_maximum_fusion.6), channel_id=1, replica_groups=mesh['grp'=8,'sub'=32] {'sub'}, dimensions={1}, use_global_device_ids=true | all-gather | bytes 118272 | tf_op jit(solution)/shard_map/all_gather | solution.py:91
  252.9 2.2 fusion.13
  255.1 33.7 %all_gather.37 = f32[7,4096]{1,0:T(8,128)S(1)} all-gather(f32[7,128]{1,0:T(8,128)S(1)} %pad_maximum_fusion.5), channel_id=1, replica_groups=mesh['grp'=8,'sub'=32] {'sub'}, dimensions={1}, use_global_device_ids=true | all-gather | bytes 118272 | tf_op jit(solution)/shard_map/all_gather | solution.py:91
  291.5 2.2 fusion.15
  293.7 30.9 %all_gather.38 = f32[7,4096]{1,0:T(8,128)S(1)} all-gather(f32[7,128]{1,0:T(8,128)S(1)} %pad_maximum_fusion.4), channel_id=1, replica_groups=mesh['grp'=8,'sub'=32] {'sub'}, dimensions={1}, use_global_device_ids=true | all-gather | bytes 118272 | tf_op jit(solution)/shard_map/all_gather | solution.py:91
  327.3 2.2 fusion.17
  329.5 33.5 %all_gather.39 = f32[7,4096]{1,0:T(8,128)S(1)} all-gather(f32[7,128]{1,0:T(8,128)S(1)} %pad_maximum_fusion.3), channel_id=1, replica_groups=mesh['grp'=8,'sub'=32] {'sub'}, dimensions={1}, use_global_device_ids=true | all-gather | bytes 118272 | tf_op jit(solution)/shard_map/all_gather | solution.py:91
  365.7 2.2 fusion.19
  367.9 30.7 %all_gather.40 = f32[7,4096]{1,0:T(8,128)S(1)} all-gather(f32[7,128]{1,0:T(8,128)S(1)} %pad_maximum_fusion.2), channel_id=1, replica_groups=mesh['grp'=8,'sub'=32] {'sub'}, dimensions={1}, use_global_device_ids=true | all-gather | bytes 118272 | tf_op jit(solution)/shard_map/all_gather | solution.py:91
  401.3 2.2 fusion.21
  403.5 33.4 %all_gather.41 = f32[7,4096]{1,0:T(8,128)S(1)} all-gather(f32[7,128]{1,0:T(8,128)S(1)} %pad_maximum_fusion.1), channel_id=1, replica_groups=mesh['grp'=8,'sub'=32] {'sub'}, dimensions={1}, use_global_device_ids=true | all-gather | bytes 118272 | tf_op jit(solution)/shard_map/all_gather | solution.py:91
  439.6 2.2 fusion.23
  441.8 31.1 %all_gather.42 = f32[7,4096]{1,0:T(8,128)S(1)} all-gather(f32[7,128]{1,0:T(8,128)S(1)} %pad_maximum_fusion), channel_id=1, replica_groups=mesh['grp'=8,'sub'=32] {'sub'}, dimensions={1}, use_global_device_ids=true | all-gather | bytes 118272 | tf_op jit(solution)/shard_map/all_gather | solution.py:91
  477.9 36.5 %all_gather.43 = f32[4,4096]{1,0:T(4,128)S(1)} all-gather(f32[4,128]{1,0:T(4,128)S(1)} %pad_maximum_fusion.9), channel_id=1, replica_groups=mesh['grp'=8,'sub'=32] {'sub'}, dimensions={1}, use_global_device_ids=true | all-gather | bytes 67584 | tf_op jit(solution)/shard_map/all_gather | solution.py:79
  514.4 8.5 %while.9 = (s32[]{:T(128)}, f32[4,3,128]{2,1,0:T(4,128)S(1)}, f32[3,4096]{1,0:T(4,128)S(1)}, f32[4,3,128]{2,1,0:T(4,128)S(1)}, f32[1,4096]{1,0:T(1,128)S(1)}, /*index=5*/s32[]{:T(128)}) while((s32[]{:T(128)}, f32[4,3,128]{2,1,0:T(4,128)S(1)}, f32[3,4096]{1,0:T(4,128)S(1)}, f32[4,3,128]{2,1,0:T(4,128)S(1)}, f32[1,4096]{1,0:T(1,128)S(1)}, ...), condition=%wide.region_45.46_spmd, body=%wide.region_42.45_spmd.sunk | while | flops 11009666 | bytes 8515149 | solution.py:34
  523.0 8.5 %while.11 = (s32[]{:T(128)}, f32[4,3,128]{2,1,0:T(4,128)S(1)}, f32[3,4096]{1,0:T(4,128)S(1)}, f32[4,3,128]{2,1,0:T(4,128)S(1)}, f32[1,4096]{1,0:T(1,128)S(1)}, /*index=5*/s32[]{:T(128)}) while((s32[]{:T(128)}, f32[4,3,128]{2,1,0:T(4,128)S(1)}, f32[3,4096]{1,0:T(4,128)S(1)}, f32[4,3,128]{2,1,0:T(4,128)S(1)}, f32[1,4096]{1,0:T(1,128)S(1)}, ...), condition=%wide.region_54.55_spmd, body=%wide.region_51.54_spmd.sunk | while | flops 11009666 | bytes 8515149 | solution.py:34
  532.1 10.4 %while.10 = (s32[]{:T(128)}, f32[4,3,1024]{2,1,0:T(4,128)S(1)}, f32[3,512]{1,0:T(4,128)S(1)}, f32[4,3,1024]{2,1,0:T(4,128)S(1)}, f32[512]{0:T(512)S(1)}, /*index=5*/s32[]{:T(128)}) while((s32[]{:T(128)}, f32[4,3,1024]{2,1,0:T(4,128)S(1)}, f32[3,512]{1,0:T(4,128)S(1)}, f32[4,3,1024]{2,1,0:T(4,128)S(1)}, f32[512]{0:T(512)S(1)}, ...), condition=%wide.region_49.50_spmd, body=%wide.region_46.49_spmd.sunk | while | flops 11006978 | bytes 8497229 | solution.py:34
  542.5 171.9 %psum.15 = f32[3,4096]{1,0:T(4,128)S(1)} all-reduce(f32[3,4096]{1,0:T(4,128)S(1)} %bitcast.92), channel_id=1, replica_groups=mesh['grp'=8,'sub'=32] {'grp','sub'}, use_global_device_ids=true, to_apply=%region_50.51 | all-reduce | flops 12288 | bytes 98304 | tf_op jit(solution)/shard_map/psum | solution.py:82
  (174 shorter events, 72.9 us)
Async XLA Ops:
  43.2 102.1 %copy-start.6 = (f32[3,128]{1,0:T(4,128)S(1)}, f32[3,128]{1,0:T(4,128)}, u32[]{:S(2)}) copy-start(f32[3,128]{1,0:T(4,128)} %param.16) | copy-start | bytes 4612
  43.2 102.1 %copy-start.3 = (f32[3,128]{1,0:T(4,128)S(1)}, f32[3,128]{1,0:T(4,128)}, u32[]{:S(2)}) copy-start(f32[3,128]{1,0:T(4,128)} %param.15) | copy-start | bytes 4612
  44.9 0.7 copy-start
  48.6 0.7 copy-start
  52.2 0.7 copy-start
  55.8 0.7 copy-start
  475.6 38.8 %copy-start.1 = (f32[3,512]{1,0:T(4,128)S(1)}, f32[3,512]{1,0:T(4,128)}, u32[]{:S(2)}) copy-start(f32[3,512]{1,0:T(4,128)} %get-tuple-element.607) | copy-start | bytes 18436
  477.8 36.6 %copy-start.5 = (f32[3,128]{1,0:T(4,128)}, f32[3,128]{1,0:T(4,128)S(1)}, u32[]{:S(2)}) copy-start(f32[3,128]{1,0:T(4,128)S(1)} %multiply_add_fusion.2) | copy-start | bytes 4612
  514.4 8.5 %copy-start.4 = (f32[3,512]{1,0:T(4,128)S(1)}, f32[3,512]{1,0:T(4,128)}, u32[]{:S(2)}) copy-start(f32[3,512]{1,0:T(4,128)} %param.19) | copy-start | bytes 18436
  542.5 172.5 %copy-start.2 = (f32[3,512]{1,0:T(4,128)}, f32[3,512]{1,0:T(4,128)S(1)}, u32[]{:S(2)}) copy-start(f32[3,512]{1,0:T(4,128)S(1)} %get-tuple-element.610) | copy-start | bytes 18436
where the time goes:
time: 725 us; the launch traced here: 715 us
  blocking collectives  625 us (86%)
  other arithmetic  86 us (12%)
    all_gather x9, blocking collectives, evaluate(): source_piece = lax.all_gather(sources, 'sub', axis=1, tiled=True)  288 us
    psum x2, blocking collectives, kick(): summed = lax.psum(partial_value, ('grp', 'sub'))  259 us
    all_gather x2, blocking collectives, kick(): gathered = lax.all_gather(stacked, 'sub', axis=1, tiled=True)  76.9 us
    reduce_sum x8, other arithmetic, rates_one_tile(): jnp.sum((closing - radial[None] * separation) * weight[None], axis=2)  17.5 us
    reduce_sum x16, other arithmetic, field_one_tile(): distance = jnp.sum(separation * separation, axis=0) + soften  17.3 us
    reduce_sum x16, other arithmetic, field_one_tile(): return jnp.sum(separation * weight[None], axis=2)  16.5 us
    reduce_sum x8, other arithmetic, rates_one_tile(): radial = 3.0 * jnp.sum(separation * closing, axis=0) / distance  16.4 us

commit v1 on v0

--- a/solution.py
+++ b/solution.py
@@ -76,7 +76,9 @@
 
     def kick(star_positions, body_positions):
         stacked = jnp.concatenate([star_positions, star_mass[None, :]], axis=0)
-        gathered = lax.all_gather(stacked, "sub", axis=1, tiled=True)
+        gathered = jnp.concatenate(
+            lax.all_to_all(jnp.stack([stacked] * lax.axis_size("sub")), "sub", 0, 0), axis=1
+        )
         galaxy_push = field(body_positions, gathered[:3], gathered[3], bridge_soft)
         partial_value = field(gathered[:3], body_positions, body_mass, bridge_soft)
         summed = lax.psum(partial_value, ("grp", "sub"))

time: 725 us -> 661 us (0.912)
  blocking collectives: 625 us -> 526 us
  waiting for transfers between devices: 0 us -> 16.9 us
  starting transfers between devices: 0 us -> 16.6 us
    all_gather x2 -> x0, blocking collectives: 76.9 us -> none  [kick(): gathered = lax.all_gather(stacked, 'sub', axis=1, tiled=True)]
    psum x2, blocking collectives: 259 us -> 236 us  [kick(): summed = lax.psum(partial_value, ('grp', 'sub'))]
    all_to_all x0 -> x2, waiting for transfers between devices: none -> 16.9 us  [kick(): lax.all_to_all(jnp.stack([stacked] * lax.axis_size('sub')), 'sub', 0, 0)]
    all_to_all x0 -> x2, starting transfers between devices: none -> 16.6 us  [kick(): lax.all_to_all(jnp.stack([stacked] * lax.axis_size('sub')), 'sub', 0, 0)]
  transfers between devices with their start and end apart: 0 -> 2, of which waited for: 0 -> 2; matrix products, arithmetic and copies ran while one was open for 0% -> 0% of each run, Pallas kernels for 0% -> 0%
where the time goes in v1:
time: 661 us; the launch traced here: 651 us
  blocking collectives  526 us (80%)
  other arithmetic  86.1 us (13%)
  waiting for transfers between devices  16.9 us (3%)
  starting transfers between devices  16.6 us (3%)
    all_gather x9, blocking collectives, evaluate(): source_piece = lax.all_gather(sources, 'sub', axis=1, tiled=True)  290 us
    psum x2, blocking collectives, kick(): summed = lax.psum(partial_value, ('grp', 'sub'))  236 us
    reduce_sum x8, other arithmetic, rates_one_tile(): jnp.sum((closing - radial[None] * separation) * weight[None], axis=2)  17.6 us
    reduce_sum x16, other arithmetic, field_one_tile(): distance = jnp.sum(separation * separation, axis=0) + soften  17.3 us
    all_to_all x2, waiting for transfers between devices, kick(): lax.all_to_all(jnp.stack([stacked] * lax.axis_size('sub')), 'sub', 0, 0)  16.9 us
    all_to_all x2, starting transfers between devices, kick(): lax.all_to_all(jnp.stack([stacked] * lax.axis_size('sub')), 'sub', 0, 0)  16.6 us
    reduce_sum x16, other arithmetic, field_one_tile(): return jnp.sum(separation * weight[None], axis=2)  16.6 us
    reduce_sum x8, other arithmetic, rates_one_tile(): radial = 3.0 * jnp.sum(separation * closing, axis=0) / distance  16.4 us
  transfers between devices with their start and end apart: 2, of which 2 were waited for; matrix products, arithmetic and copies ran while one was open for 0% of the time, Pallas kernels for 0%

profile of v1, /device:TPU:1, one launch (start us, length us, event | category | flops | bytes accessed | tf_op | source)
XLA Modules:
  0.0 651.4 jit_solution(15166992775129627120)
XLA Ops:
  2.6 11.9 %all-to-all-start = ((f32[32,4,128]{2,1,0:T(4,128)}), f32[32,4,128]{2,1,0:T(4,128)S(1)}, u32[]{:S(2)}, u32[]{:S(2)}) async-start(f32[32,4,128]{2,1,0:T(4,128)} %stack.4), calls=%async_computation | async-start | bytes 131072 | tf_op jit(solution)/shard_map/all_to_all | solution.py:80
  15.3 8.1 %all-to-all-done = f32[32,4,128]{2,1,0:T(4,128)S(1)} async-done(((f32[32,4,128]{2,1,0:T(4,128)}), f32[32,4,128]{2,1,0:T(4,128)S(1)}, u32[]{:S(2)}, u32[]{:S(2)}) %all-to-all-start) | async-done | bytes 65568 | tf_op jit(solution)/shard_map/all_to_all | solution.py:80
  23.5 14.6 %while.8 = (s32[]{:T(128)}, f32[4,3,1024]{2,1,0:T(4,128)S(1)}, f32[3,512]{1,0:T(4,128)}, f32[4,3,1024]{2,0,1:T(4,128)S(1)}, f32[512]{0:T(512)S(1)}, /*index=5*/s32[]{:T(128)}) while((s32[]{:T(128)}, f32[4,3,1024]{2,1,0:T(4,128)S(1)}, f32[3,512]{1,0:T(4,128)}, f32[4,3,1024]{2,0,1:T(4,128)S(1)}, f32[512]{0:T(512)S(1)}, ...), condition=%wide.region_4.5_spmd, body=%wide.region_1.4_spmd.sunk | while | flops 11006978 | bytes 8546417 | solution.py:34
  38.0 75.6 %psum.14 = f32[3,4096]{1,0:T(4,128)S(1)} all-reduce(f32[3,4096]{1,0:T(4,128)S(1)} %bitcast.102), channel_id=1, replica_groups=mesh['grp'=8,'sub'=32] {'grp','sub'}, use_global_device_ids=true, to_apply=%region_5.6 | all-reduce | flops 12288 | bytes 98304 | tf_op jit(solution)/shard_map/psum | solution.py:84
  113.7 32.0 %all_gather.27 = f32[7,4096]{1,0:T(8,128)S(1)} all-gather(f32[7,128]{1,0:T(8,128)S(1)} %pad_maximum_fusion.8), channel_id=1, replica_groups=mesh['grp'=8,'sub'=32] {'sub'}, dimensions={1}, use_global_device_ids=true | all-gather | bytes 118272 | tf_op jit(solution)/shard_map/all_gather | solution.py:93
  150.4 31.4 %all_gather.28 = f32[7,4096]{1,0:T(8,128)S(1)} all-gather(f32[7,128]{1,0:T(8,128)S(1)} %pad_maximum_fusion.7), channel_id=1, replica_groups=mesh['grp'=8,'sub'=32] {'sub'}, dimensions={1}, use_global_device_ids=true | all-gather | bytes 118272 | tf_op jit(solution)/shard_map/all_gather | solution.py:93
  184.5 2.2 fusion.11
  186.7 33.0 %all_gather.29 = f32[7,4096]{1,0:T(8,128)S(1)} all-gather(f32[7,128]{1,0:T(8,128)S(1)} %pad_maximum_fusion.6), channel_id=1, replica_groups=mesh['grp'=8,'sub'=32] {'sub'}, dimensions={1}, use_global_device_ids=true | all-gather | bytes 118272 | tf_op jit(solution)/shard_map/all_gather | solution.py:93
  222.4 2.2 fusion.13
  224.7 31.7 %all_gather.30 = f32[7,4096]{1,0:T(8,128)S(1)} all-gather(f32[7,128]{1,0:T(8,128)S(1)} %pad_maximum_fusion.5), channel_id=1, replica_groups=mesh['grp'=8,'sub'=32] {'sub'}, dimensions={1}, use_global_device_ids=true | all-gather | bytes 118272 | tf_op jit(solution)/shard_map/all_gather | solution.py:93
  259.1 2.2 fusion.15
  261.3 32.7 %all_gather.31 = f32[7,4096]{1,0:T(8,128)S(1)} all-gather(f32[7,128]{1,0:T(8,128)S(1)} %pad_maximum_fusion.4), channel_id=1, replica_groups=mesh['grp'=8,'sub'=32] {'sub'}, dimensions={1}, use_global_device_ids=true | all-gather | bytes 118272 | tf_op jit(solution)/shard_map/all_gather | solution.py:93
  298.9 31.3 %all_gather.32 = f32[7,4096]{1,0:T(8,128)S(1)} all-gather(f32[7,128]{1,0:T(8,128)S(1)} %pad_maximum_fusion.3), channel_id=1, replica_groups=mesh['grp'=8,'sub'=32] {'sub'}, dimensions={1}, use_global_device_ids=true | all-gather | bytes 118272 | tf_op jit(solution)/shard_map/all_gather | solution.py:93
  332.9 2.2 fusion.19
  335.1 32.5 %all_gather.33 = f32[7,4096]{1,0:T(8,128)S(1)} all-gather(f32[7,128]{1,0:T(8,128)S(1)} %pad_maximum_fusion.2), channel_id=1, replica_groups=mesh['grp'=8,'sub'=32] {'sub'}, dimensions={1}, use_global_device_ids=true | all-gather | bytes 118272 | tf_op jit(solution)/shard_map/all_gather | solution.py:93
  372.5 31.7 %all_gather.34 = f32[7,4096]{1,0:T(8,128)S(1)} all-gather(f32[7,128]{1,0:T(8,128)S(1)} %pad_maximum_fusion.1), channel_id=1, replica_groups=mesh['grp'=8,'sub'=32] {'sub'}, dimensions={1}, use_global_device_ids=true | all-gather | bytes 118272 | tf_op jit(solution)/shard_map/all_gather | solution.py:93
  409.2 33.6 %all_gather.35 = f32[7,4096]{1,0:T(8,128)S(1)} all-gather(f32[7,128]{1,0:T(8,128)S(1)} %pad_maximum_fusion), channel_id=1, replica_groups=mesh['grp'=8,'sub'=32] {'sub'}, dimensions={1}, use_global_device_ids=true | all-gather | bytes 118272 | tf_op jit(solution)/shard_map/all_gather | solution.py:93
  442.8 8.5 %while.9 = (s32[]{:T(128)}, f32[4,3,128]{2,1,0:T(4,128)S(1)}, f32[3,4096]{1,0:T(4,128)S(1)}, f32[4,3,128]{2,1,0:T(4,128)S(1)}, f32[1,4096]{1,0:T(1,128)S(1)}, /*index=5*/s32[]{:T(128)}) while((s32[]{:T(128)}, f32[4,3,128]{2,1,0:T(4,128)S(1)}, f32[3,4096]{1,0:T(4,128)S(1)}, f32[4,3,128]{2,1,0:T(4,128)S(1)}, f32[1,4096]{1,0:T(1,128)S(1)}, ...), condition=%wide.region_45.46_spmd, body=%wide.region_42.45_spmd.sunk | while | flops 11009666 | bytes 8515157 | solution.py:34
  454.0 2.3 fusion.25
  456.9 4.7 all-to-all-start.1
  461.7 8.8 %all-to-all-done.1 = f32[32,4,128]{2,1,0:T(4,128)S(1)} async-done(((f32[32,4,128]{2,1,0:T(4,128)}), f32[32,4,128]{2,1,0:T(4,128)S(1)}, u32[]{:S(2)}, u32[]{:S(2)}) %all-to-all-start.1) | async-done | bytes 65568 | tf_op jit(solution)/shard_map/all_to_all | solution.py:80
  470.6 8.5 %while.11 = (s32[]{:T(128)}, f32[4,3,128]{2,1,0:T(4,128)S(1)}, f32[3,4096]{1,0:T(4,128)S(1)}, f32[4,3,128]{2,1,0:T(4,128)S(1)}, f32[1,4096]{1,0:T(1,128)S(1)}, /*index=5*/s32[]{:T(128)}) while((s32[]{:T(128)}, f32[4,3,128]{2,1,0:T(4,128)S(1)}, f32[3,4096]{1,0:T(4,128)S(1)}, f32[4,3,128]{2,1,0:T(4,128)S(1)}, f32[1,4096]{1,0:T(1,128)S(1)}, ...), condition=%wide.region_54.55_spmd, body=%wide.region_51.54_spmd.sunk | while | flops 11009666 | bytes 8515157 | solution.py:34
  479.8 10.5 %while.10 = (s32[]{:T(128)}, f32[4,3,1024]{2,1,0:T(4,128)S(1)}, f32[3,512]{1,0:T(4,128)S(1)}, f32[4,3,1024]{2,0,1:T(4,128)S(1)}, f32[512]{0:T(512)S(1)}, /*index=5*/s32[]{:T(128)}) while((s32[]{:T(128)}, f32[4,3,1024]{2,1,0:T(4,128)S(1)}, f32[3,512]{1,0:T(4,128)S(1)}, f32[4,3,1024]{2,0,1:T(4,128)S(1)}, f32[512]{0:T(512)S(1)}, ...), condition=%wide.region_49.50_spmd, body=%wide.region_46.49_spmd.sunk | while | flops 11006978 | bytes 8521813 | solution.py:34
  490.3 160.1 %psum.15 = f32[3,4096]{1,0:T(4,128)S(1)} all-reduce(f32[3,4096]{1,0:T(4,128)S(1)} %bitcast.101), channel_id=1, replica_groups=mesh['grp'=8,'sub'=32] {'grp','sub'}, use_global_device_ids=true, to_apply=%region_50.51 | all-reduce | flops 12288 | bytes 98304 | tf_op jit(solution)/shard_map/psum | solution.py:84
  (192 shorter events, 78.8 us)
Async XLA Ops:
  2.6 20.7 %all-to-all-start = ((f32[32,4,128]{2,1,0:T(4,128)}), f32[32,4,128]{2,1,0:T(4,128)S(1)}, u32[]{:S(2)}, u32[]{:S(2)}) async-start(f32[32,4,128]{2,1,0:T(4,128)} %stack.4), calls=%async_computation | async-start | bytes 131072 | tf_op jit(solution)/shard_map/all_to_all | solution.py:80
  23.4 90.2 %copy-start.6 = (f32[3,128]{1,0:T(4,128)S(1)}, f32[3,128]{1,0:T(4,128)}, u32[]{:S(2)}) copy-start(f32[3,128]{1,0:T(4,128)} %param.16) | copy-start | bytes 4612
  23.5 90.2 %copy-start.3 = (f32[3,128]{1,0:T(4,128)S(1)}, f32[3,128]{1,0:T(4,128)}, u32[]{:S(2)}) copy-start(f32[3,128]{1,0:T(4,128)} %param.15) | copy-start | bytes 4612
  25.2 0.7 copy-start
  28.8 0.7 copy-start
  32.4 0.7 copy-start
  36.1 0.7 copy-start
  407.0 35.9 %copy-start.1 = (f32[3,512]{1,0:T(4,128)S(1)}, f32[3,512]{1,0:T(4,128)}, u32[]{:S(2)}) copy-start(f32[3,512]{1,0:T(4,128)} %get-tuple-element.639) | copy-start | bytes 18436
  454.0 7.7 %copy-start.4 = (f32[3,512]{1,0:T(4,128)S(1)}, f32[3,512]{1,0:T(4,128)}, u32[]{:S(2)}) copy-start(f32[3,512]{1,0:T(4,128)} %param.19) | copy-start | bytes 18436
  456.3 14.3 %copy-start.5 = (f32[3,128]{1,0:T(4,128)}, f32[3,128]{1,0:T(4,128)S(1)}, u32[]{:S(2)}) copy-start(f32[3,128]{1,0:T(4,128)S(1)} %multiply_add_fusion.2) | copy-start | bytes 4612
  456.9 13.6 %all-to-all-start.1 = ((f32[32,4,128]{2,1,0:T(4,128)}), f32[32,4,128]{2,1,0:T(4,128)S(1)}, u32[]{:S(2)}, u32[]{:S(2)}) async-start(f32[32,4,128]{2,1,0:T(4,128)} %stack.5), calls=%async_computation.1 | async-start | bytes 131072 | tf_op jit(solution)/shard_map/all_to_all | solution.py:80
  490.3 160.7 %copy-start.2 = (f32[3,512]{1,0:T(4,128)}, f32[3,512]{1,0:T(4,128)S(1)}, u32[]{:S(2)}) copy-start(f32[3,512]{1,0:T(4,128)S(1)} %get-tuple-element.642) | copy-start | bytes 18436
